TPU v7x, 32 devices: a whole 2x2x4 slice. The times are simulated.
32 devices in a mesh: row: 8 (over y, x, core), col: 4 (over z).
Axes of the slice: x: 2, y: 2, z: 4, core: 2. Of those that a mesh axis runs over, the one named last changes fastest.
Arguments:
- base_weights: bfloat16 [2, 8192, 28672], P(None, 'row', 'col'), may hold values from -6 to 6
- left_factors: bfloat16 [2, 8192, 4, 128], P(None, 'row', 'col'), may hold values from -6 to 6
- right_factors: bfloat16 [2, 4, 128, 28672], P(None, 'col', None, 'row'), may hold values from -6 to 6
- client_adapter_ranks: int32 [4], replicated, may hold values from 16 to 128, as said below
- step_counts: int32 [4], replicated, may hold values from 100 to 1000
- worker_slot: int32 [4], replicated, may hold values from 0 to 3, each once
Outputs:
- merged: bfloat16 [2, 8192, 28672], P(None, 'row', 'col')
Inputs may be any that keep to these rules, and one draw needn't show every extreme that they name: `client_adapter_ranks`: each rank is a multiple of 16; the ranks sum to 256; at least one rank equals 128. `worker_slot`: a permutation: every slot holds exactly one worker's factors.
All inputs are finite; a program needn't handle non-finite values.
Results may differ from a plain program's by a relative error of at most 0.0045.
Values may be sent and summed in bfloat16 or wider, within the bound.
No kernel may reach another device: no remote copies, remote signals or barrier semaphores. Data moves between devices by JAX's collectives and lax.ppermute only.
A program may use at most 192 MiB of HBM per device.

v0:
```python
import jax
import jax.numpy as jnp
from jax import lax
from jax.sharding import PartitionSpec as P

ADAPTER_ALPHA = 32


def slot_tables(client_adapter_ranks, step_counts, worker_slot):
    workers = client_adapter_ranks.shape[0]
    slot_ids = jnp.arange(workers, dtype=jnp.int32)
    slot_hot = worker_slot[:, None] == slot_ids[None, :]
    rank_slot = jnp.sum(jnp.where(slot_hot, client_adapter_ranks[:, None], 0), axis=0)
    counts = step_counts.astype(jnp.float32)
    per_step_portion = counts / jnp.sum(counts)
    client_scale = ADAPTER_ALPHA * per_step_portion / client_adapter_ranks.astype(jnp.float32)
    slot_scale_factor = jnp.sum(jnp.where(slot_hot, client_scale[:, None], 0.0), axis=0)
    return (rank_slot, slot_scale_factor)


def merge_tile(base_tile, left_piece, right_piece):
    tile_rows = base_tile.shape[0]
    rank_cap = right_piece.shape[1]
    block_width = right_piece.shape[2]
    row_count = lax.axis_size("row")
    col_count = lax.axis_size("col")
    row_ratio = row_count // col_count
    left_all = lax.all_gather(left_piece, "col", axis=1, tiled=True)
    sub_width = block_width // row_count
    split_view = right_piece.reshape(1, rank_cap, row_count, sub_width)
    spread = lax.all_to_all(split_view, "row", split_axis=2, concat_axis=2, tiled=True)
    pair_view = spread.reshape(1, rank_cap, col_count, row_ratio, sub_width)
    slot_pieces = lax.all_to_all(pair_view, "col", split_axis=2, concat_axis=0, tiled=True)
    join_view = slot_pieces.reshape(col_count, rank_cap, row_ratio, 1, sub_width)
    joined = lax.all_gather(join_view, "row", axis=3, tiled=True)
    right_cols = joined.reshape(col_count, rank_cap, row_ratio * block_width)
    left_flat = left_all.reshape(tile_rows, -1)
    right_flat = right_cols.reshape(left_flat.shape[1], -1)
    delta_tile = jnp.dot(left_flat, right_flat, preferred_element_type=jnp.float32)
    return (base_tile.astype(jnp.float32) + delta_tile).astype(jnp.bfloat16)


def body(base_weights, left_factors, right_factors, client_adapter_ranks, step_counts, worker_slot):
    workers = client_adapter_ranks.shape[0]
    rank_cap = right_factors.shape[2]
    rank_slot, slot_scale_factor = slot_tables(client_adapter_ranks, step_counts, worker_slot)
    own_hot = jnp.arange(workers, dtype=jnp.int32) == lax.axis_index("col")
    own_rank = jnp.sum(jnp.where(own_hot, rank_slot, 0))
    own_scale = jnp.sum(jnp.where(own_hot, slot_scale_factor, 0.0))
    rank_scale = jnp.where(jnp.arange(rank_cap, dtype=jnp.int32) < own_rank, own_scale, 0.0)
    scaled_right = (right_factors.astype(jnp.float32) * rank_scale[None, None, :, None]).astype(
        jnp.bfloat16
    )
    merged = [
        merge_tile(base_weights[number], left_factors[number], scaled_right[number])
        for number in range(base_weights.shape[0])
    ]
    return jnp.stack(merged)


def solution(mesh):
    return jax.shard_map(
        body,
        mesh=mesh,
        in_specs=(
            P(None, "row", "col"),
            P(None, "row", "col", None),
            P(None, "col", None, "row"),
            P(),
            P(),
            P(),
        ),
        out_specs=P(None, "row", "col"),
        check_vma=False,
    )
```

profile of v0, /device:TPU:0, one launch (start us, length us, event | category | flops | bytes accessed | tf_op | source)
XLA Modules:
  0.0 342.5 jit_solution(10027888626244682523)
XLA Ops:
  6.5 0.0 all-gather.11.cloned.1.call-start
  6.5 1.9 fusion.8
  8.4 0.0 all-gather.11.cloned.1.call-update
  8.4 1.3 convert_reduce_fusion
  9.7 1.3 convert_divide_fusion
  11.0 0.8 select_reduce_fusion.1
  11.8 0.7 select_reduce_fusion
  12.5 0.6 fusion.5
  13.1 0.7 fusion.4
  13.8 2.9 copy.33
  16.7 1.3 compare_select_fusion
  18.1 0.4 multiply_convert_fusion
  18.4 1.0 fusion.7
  19.5 5.2 %all-to-all-start = ((bf16[1,128,8,448]{1,3,0,2:T(8,128)(2,1)}), bf16[1,128,8,448]{1,3,0,2:T(8,128)(2,1)S(1)}, u32[]{:S(2)}, u32[]{:S(2)}) async-start(bf16[1,128,8,448]{1,3,0,2:T(8,128)(2,1)} %bitcast.2), calls=%async_computation | async-start | bytes 1835008 | tf_op jit(solution)/shard_map/all_to_all | solution.py:31
  24.7 0.0 all-gather.15.cloned.1.call-start
  24.7 0.7 all-gather.15.cloned.1.call-update
  25.4 0.0 all-gather.9.cloned.1.call-start
  25.5 13.2 %all-to-all-done = bf16[1,128,8,448]{1,3,0,2:T(8,128)(2,1)S(1)} async-done(((bf16[1,128,8,448]{1,3,0,2:T(8,128)(2,1)}), bf16[1,128,8,448]{1,3,0,2:T(8,128)(2,1)S(1)}, u32[]{:S(2)}, u32[]{:S(2)}) %all-to-all-start) | async-done | bytes 917536 | tf_op jit(solution)/shard_map/all_to_all | solution.py:31
  38.6 41.8 %all_to_all.40 = bf16[1,128,4,2,448]{1,4,3,0,2:T(8,128)(2,1)} all-to-all(bf16[1,128,4,2,448]{1,4,3,0,2:T(8,128)(2,1)S(1)} %bitcast.63), channel_id=1, replica_groups=mesh['row'=8,'col'=4] {'col'}, dimensions={2} | all-to-all | bytes 1835008 | tf_op jit(solution)/shard_map/all_to_all | solution.py:33
  80.5 0.0 all-gather.9.cloned.1.call-update
  80.5 0.0 all-gather.13.cloned.1.call-start
  80.6 23.2 %all_to_all.41 = bf16[1,128,8,448]{1,3,0,2:T(8,128)(2,1)S(1)} all-to-all(bf16[1,128,8,448]{1,3,0,2:T(8,128)(2,1)S(1)} %bitcast.60), channel_id=1, replica_groups=mesh['row'=8,'col'=4] {'row'}, dimensions={2} | all-to-all | bytes 1835008 | tf_op jit(solution)/shard_map/all_to_all | solution.py:31
  103.8 25.3 %all_to_all.42 = bf16[1,128,4,2,448]{1,4,3,0,2:T(8,128)(2,1)} all-to-all(bf16[1,128,4,2,448]{1,4,3,0,2:T(8,128)(2,1)S(1)} %bitcast.64), channel_id=1, replica_groups=mesh['row'=8,'col'=4] {'col'}, dimensions={2} | all-to-all | bytes 1835008 | tf_op jit(solution)/shard_map/all_to_all | solution.py:33
  129.1 0.0 all-gather.13.cloned.1.call-update
  129.1 22.1 %fusion.6 = (bf16[1,1024,7168]{2,1,0:T(8,128)(2,1)}, bf16[1,1024,7168]{2,1,0:T(8,128)(2,1)}) fusion(bf16[2,1024,7168]{2,1,0:T(8,128)(2,1)} %param.6), kind=kLoop, calls=%fused_computation.18 | loop fusion | bytes 58720256 | tf_op jit(solution)/shard_map/slice | solution.py:55
  151.2 19.5 %copy.46 = bf16[1,1024,7168]{1,2,0:T(8,128)(2,1)} copy(bf16[1,1024,7168]{2,1,0:T(8,128)(2,1)} %get-tuple-element.5) | data formatting | bytes 29360128
  170.7 19.9 %copy.47 = bf16[1,1024,7168]{1,2,0:T(8,128)(2,1)} copy(bf16[1,1024,7168]{2,1,0:T(8,128)(2,1)} %get-tuple-element.6) | data formatting | bytes 29360128
  190.6 0.0 all-gather.11.cloned.1.call-done
  190.6 1.5 copy.38
  192.1 0.0 all-gather.15.cloned.1.call-done
  192.1 1.5 copy.44
  193.6 0.0 all-gather.9.cloned.1.call-done
  193.7 18.8 %copy.36 = bf16[4,1,128,1,2,3584]{5,4,2,0,3,1:T(2,128)(2,1)} copy(bf16[4,1,128,1,2,3584]{2,5,4,0,3,1:T(8,128)(2,1)} %all-gather.9.cloned.1.call-done) | data formatting | bytes 14680064 | tf_op jit(solution)/shard_map/all_gather | solution.py:35
  212.4 7.8 %copy.48 = bf16[64,8,2,3584]{3,1,2,0:T(8,128)(2,1)} copy(bf16[64,8,2,3584]{3,2,1,0:T(2,128)(2,1)} %bitcast.56) | data formatting | bytes 14680064
  220.3 0.0 all-gather.13.cloned.1.call-done
  220.3 18.8 %copy.42 = bf16[4,1,128,1,2,3584]{5,4,2,0,3,1:T(2,128)(2,1)} copy(bf16[4,1,128,1,2,3584]{2,5,4,0,3,1:T(8,128)(2,1)} %all-gather.13.cloned.1.call-done) | data formatting | bytes 14680064 | tf_op jit(solution)/shard_map/all_gather | solution.py:35
  239.0 7.8 %copy.49 = bf16[64,8,2,3584]{3,1,2,0:T(8,128)(2,1)} copy(bf16[64,8,2,3584]{3,2,1,0:T(2,128)(2,1)} %bitcast.57) | data formatting | bytes 14680064
  246.8 16.3 %fusion.2 = bf16[1,1024,7168]{1,2,0:T(8,128)(2,1)} fusion(bf16[512,7168]{1,0:T(8,128)(2,1)} %bitcast.58, bf16[1024,512]{0,1:T(8,128)(2,1)S(1)} %bitcast.65, bf16[1,1024,7168]{1,2,0:T(8,128)(2,1)} %copy.46), kind=kOutput, calls=%fused_computation.5 | convolution fusion | flops 7538212864 | bytes 37748736 | tf_op jit(solution)/shard_map/dot_general | solution.py:39
  263.1 16.5 %fusion.3 = bf16[1,1024,7168]{1,2,0:T(8,128)(2,1)} fusion(bf16[512,7168]{1,0:T(8,128)(2,1)} %bitcast.59, bf16[1024,512]{0,1:T(8,128)(2,1)S(1)} %bitcast.66, bf16[1,1024,7168]{1,2,0:T(8,128)(2,1)} %copy.47), kind=kOutput, calls=%fused_computation.6 | convolution fusion | flops 7538212864 | bytes 37748736 | tf_op jit(solution)/shard_map/dot_general | solution.py:39
  279.6 20.1 %pad_maximum_fusion = bf16[2,1024,7168]{1,2,0:T(8,128)(2,1)} fusion(bf16[1,1024,7168]{1,2,0:T(8,128)(2,1)} %fusion.3, bf16[1,1024,7168]{1,2,0:T(8,128)(2,1)} %fusion.2), kind=kLoop, calls=%fused_computation | loop fusion | flops 14680064 | bytes 58720256 | tf_op jit(solution)/shard_map/stack | solution.py:58
  299.7 36.2 %copy.45 = bf16[2,1024,7168]{2,1,0:T(8,128)(2,1)} copy(bf16[2,1024,7168]{1,2,0:T(8,128)(2,1)} %pad_maximum_fusion) | data formatting | bytes 58720256 | tf_op jit(solution)/shard_map/stack | solution.py:58
Async XLA Ops:
  6.5 184.1 %all-gather.11.cloned.1.call-start = ((), (), s32[]{:S(2)}) async-start(), calls=%async_computation.5 | async-start | bytes 1310720 | tf_op jit(solution)/shard_map/all_gather | solution.py:28
  19.5 19.2 %all-to-all-start = ((bf16[1,128,8,448]{1,3,0,2:T(8,128)(2,1)}), bf16[1,128,8,448]{1,3,0,2:T(8,128)(2,1)S(1)}, u32[]{:S(2)}, u32[]{:S(2)}) async-start(bf16[1,128,8,448]{1,3,0,2:T(8,128)(2,1)} %bitcast.2), calls=%async_computation | async-start | bytes 1835008 | tf_op jit(solution)/shard_map/all_to_all | solution.py:31
  24.7 167.5 %all-gather.15.cloned.1.call-start = ((), (), s32[]{:S(2)}) async-start(), calls=%async_computation.7 | async-start | bytes 1310720 | tf_op jit(solution)/shard_map/all_gather | solution.py:28
  25.4 168.2 %all-gather.9.cloned.1.call-start = ((), (), s32[]{:S(2)}) async-start(), calls=%async_computation.4 | async-start | bytes 8257536 | tf_op jit(solution)/shard_map/all_gather | solution.py:35
  80.5 139.8 %all-gather.13.cloned.1.call-start = ((), (), s32[]{:S(2)}) async-start(), calls=%async_computation.6 | async-start | bytes 8257536 | tf_op jit(solution)/shard_map/all_gather | solution.py:35
Sparse Core Ops, SparseCore 0:
  8.9 30.6 all-gather.10
  41.2 39.3 all-gather.14
  82.5 52.3 all-gather.8
  136.7 49.8 all-gather.12
where the time goes:
time: 346 us; the launch traced here: 342 us
  local copies, waits for them, and re-layouts  160 us (46%)
  blocking collectives  90.3 us (26%)
  matrix products  32.8 us (9%)
  other arithmetic  27.2 us (8%)
  waiting for transfers between devices  14 us (4%)
  between operations  13.2 us (4%)
  starting transfers between devices  5.32 us (2%)
    all_to_all x2, blocking collectives, merge_tile(): lax.all_to_all(pair_view, 'col', split_axis=2, concat_axis=0, tiled=True)  67.1 us
    unnamed x5, local copies, waits for them, and re-layouts  57.9 us
    all_gather x2, local copies, waits for them, and re-layouts, merge_tile(): joined = lax.all_gather(join_view, 'row', axis=3, tiled=True)  37.6 us
    another operation x1, local copies, waits for them, and re-layouts, body(): return jnp.stack(merged)  36.2 us
    dot_general x2, matrix products, merge_tile(): jnp.dot(left_flat, right_flat, preferred_element_type=jnp.float32)  32.8 us
    all_to_all x1, blocking collectives, merge_tile(): lax.all_to_all(split_view, 'row', split_axis=2, concat_axis=2, tiled=True)  23.2 us
    slice x1, local copies, waits for them, and re-layouts, body(): base_weights[number]  22.1 us
    another operation x1, other arithmetic, body(): return jnp.stack(merged)  20.1 us
  transfers between devices with their start and end apart: 5, of which 1 were waited for; matrix products, arithmetic and copies ran while one was open for 30% of the time, Pallas kernels for 0%

commit v1 on v0

--- a/solution.py
+++ b/solution.py
@@ -32,7 +32,7 @@
     pair_view = spread.reshape(1, rank_cap, col_count, row_ratio, sub_width)
     slot_pieces = lax.all_to_all(pair_view, "col", split_axis=2, concat_axis=0, tiled=True)
     join_view = slot_pieces.reshape(col_count, rank_cap, row_ratio, 1, sub_width)
-    joined = lax.all_gather(join_view, "row", axis=3, tiled=True)
+    joined = jnp.concatenate(lax.all_gather(join_view, "row"), axis=3)
     right_cols = joined.reshape(col_count, rank_cap, row_ratio * block_width)
     left_flat = left_all.reshape(tile_rows, -1)
     right_flat = right_cols.reshape(left_flat.shape[1], -1)

time: 346 us -> 317 us (0.916)
  local copies, waits for them, and re-layouts: 160 us -> 131 us
    unnamed x5 -> x3, local copies, waits for them, and re-layouts: 57.9 us -> 42.4 us
    all_gather x2, local copies, waits for them, and re-layouts: 37.6 us -> 24.6 us  [merge_tile(): joined = jnp.concatenate(lax.all_gather(join_view, 'row'), axis=3)]
  transfers between devices with their start and end apart: 5 -> 5, of which waited for: 1 -> 1; matrix products, arithmetic and copies ran while one was open for 30% -> 28% of each run, Pallas kernels for 0% -> 0%
where the time goes in v1:
time: 317 us; the launch traced here: 314 us
  local copies, waits for them, and re-layouts  131 us (41%)
  blocking collectives  90.3 us (28%)
  matrix products  33.1 us (10%)
  other arithmetic  27.2 us (9%)
  waiting for transfers between devices  14 us (4%)
  between operations  13.2 us (4%)
  starting transfers between devices  5.32 us (2%)
    all_to_all x2, blocking collectives, merge_tile(): lax.all_to_all(pair_view, 'col', split_axis=2, concat_axis=0, tiled=True)  67.1 us
    unnamed x3, local copies, waits for them, and re-layouts  42.4 us
    another operation x1, local copies, waits for them, and re-layouts, body(): return jnp.stack(merged)  36.2 us
    dot_general x2, matrix products, merge_tile(): jnp.dot(left_flat, right_flat, preferred_element_type=jnp.float32)  33.1 us
    all_gather x2, local copies, waits for them, and re-layouts, merge_tile(): joined = jnp.concatenate(lax.all_gather(join_view, 'row'), axis=3)  24.6 us
    all_to_all x1, blocking collectives, merge_tile(): lax.all_to_all(split_view, 'row', split_axis=2, concat_axis=2, tiled=True)  23.2 us
    slice x1, local copies, waits for them, and re-layouts, body(): base_weights[number]  22.1 us
    another operation x1, other arithmetic, body(): return jnp.stack(merged)  20.1 us
  transfers between devices with their start and end apart: 5, of which 1 were waited for; matrix products, arithmetic and copies ran while one was open for 28% of the time, Pallas kernels for 0%

profile of v1, /device:TPU:0, one launch (start us, length us, event | category | flops | bytes accessed | tf_op | source)
XLA Modules:
  0.0 314.4 jit_solution(13219718769815961983)
XLA Ops:
  6.5 0.0 all-gather.11.cloned.1.call-start
  6.5 1.9 fusion.12
  8.4 0.0 all-gather.11.cloned.1.call-update
  8.4 1.3 convert_reduce_fusion
  9.7 1.3 convert_divide_fusion
  11.0 0.8 select_reduce_fusion.1
  11.8 0.7 select_reduce_fusion
  12.5 0.6 fusion.9
  13.1 0.7 fusion.8
  13.8 2.9 copy.35
  16.7 1.3 compare_select_fusion
  18.1 0.4 multiply_convert_fusion
  18.4 1.0 fusion.11
  19.5 5.2 %all-to-all-start = ((bf16[1,128,8,448]{1,3,0,2:T(8,128)(2,1)}), bf16[1,128,8,448]{1,3,0,2:T(8,128)(2,1)S(1)}, u32[]{:S(2)}, u32[]{:S(2)}) async-start(bf16[1,128,8,448]{1,3,0,2:T(8,128)(2,1)} %bitcast.2), calls=%async_computation | async-start | bytes 1835008 | tf_op jit(solution)/shard_map/all_to_all | solution.py:31
  24.7 0.0 all-gather.15.cloned.1.call-start
  24.7 0.7 all-gather.15.cloned.1.call-update
  25.4 0.0 all-gather.9.cloned.1.call-start
  25.5 13.2 %all-to-all-done = bf16[1,128,8,448]{1,3,0,2:T(8,128)(2,1)S(1)} async-done(((bf16[1,128,8,448]{1,3,0,2:T(8,128)(2,1)}), bf16[1,128,8,448]{1,3,0,2:T(8,128)(2,1)S(1)}, u32[]{:S(2)}, u32[]{:S(2)}) %all-to-all-start) | async-done | bytes 917536 | tf_op jit(solution)/shard_map/all_to_all | solution.py:31
  38.6 41.8 %all_to_all.40 = bf16[1,128,4,2,448]{1,4,3,0,2:T(8,128)(2,1)} all-to-all(bf16[1,128,4,2,448]{1,4,3,0,2:T(8,128)(2,1)S(1)} %bitcast.75), channel_id=1, replica_groups=mesh['row'=8,'col'=4] {'col'}, dimensions={2} | all-to-all | bytes 1835008 | tf_op jit(solution)/shard_map/all_to_all | solution.py:33
  80.5 0.0 all-gather.9.cloned.1.call-update
  80.5 0.0 all-gather.13.cloned.1.call-start
  80.6 23.2 %all_to_all.41 = bf16[1,128,8,448]{1,3,0,2:T(8,128)(2,1)S(1)} all-to-all(bf16[1,128,8,448]{1,3,0,2:T(8,128)(2,1)S(1)} %bitcast.72), channel_id=1, replica_groups=mesh['row'=8,'col'=4] {'row'}, dimensions={2} | all-to-all | bytes 1835008 | tf_op jit(solution)/shard_map/all_to_all | solution.py:31
  103.8 25.3 %all_to_all.42 = bf16[1,128,4,2,448]{1,4,3,0,2:T(8,128)(2,1)} all-to-all(bf16[1,128,4,2,448]{1,4,3,0,2:T(8,128)(2,1)S(1)} %bitcast.76), channel_id=1, replica_groups=mesh['row'=8,'col'=4] {'col'}, dimensions={2} | all-to-all | bytes 1835008 | tf_op jit(solution)/shard_map/all_to_all | solution.py:33
  129.1 0.0 all-gather.13.cloned.1.call-update
  129.1 22.1 %fusion.10 = (bf16[1,1024,7168]{2,1,0:T(8,128)(2,1)}, bf16[1,1024,7168]{2,1,0:T(8,128)(2,1)}) fusion(bf16[2,1024,7168]{2,1,0:T(8,128)(2,1)} %param.6), kind=kLoop, calls=%fused_computation.22 | loop fusion | bytes 58720256 | tf_op jit(solution)/shard_map/slice | solution.py:55
  151.2 19.5 %copy.50 = bf16[1,1024,7168]{1,2,0:T(8,128)(2,1)} copy(bf16[1,1024,7168]{2,1,0:T(8,128)(2,1)} %get-tuple-element.5) | data formatting | bytes 29360128
  170.7 20.0 %copy.51 = bf16[1,1024,7168]{1,2,0:T(8,128)(2,1)} copy(bf16[1,1024,7168]{2,1,0:T(8,128)(2,1)} %get-tuple-element.6) | data formatting | bytes 29360128
  190.7 0.0 all-gather.11.cloned.1.call-done
  190.7 1.5 copy.41
  192.2 0.0 all-gather.15.cloned.1.call-done
  192.2 1.7 copy.48
  193.9 0.0 all-gather.9.cloned.1.call-done
  193.9 12.2 %copy.39 = bf16[8,4,128,2,1,448]{2,1,5,0,3,4:T(4,128)(2,1)} copy(bf16[8,4,128,2,1,448]{2,5,3,1,0,4:T(8,128)(2,1)} %bitcast.68) | data formatting | bytes 14680064 | tf_op jit(solution)/shard_map/all_gather | solution.py:35
  206.1 0.0 all-gather.13.cloned.1.call-done
  206.1 12.5 %copy.46 = bf16[8,4,128,2,1,448]{2,1,5,0,3,4:T(4,128)(2,1)} copy(bf16[8,4,128,2,1,448]{2,5,3,1,0,4:T(8,128)(2,1)} %bitcast.69) | data formatting | bytes 14680064 | tf_op jit(solution)/shard_map/all_gather | solution.py:35
  218.6 16.4 %fusion.2 = bf16[1,1024,7168]{1,2,0:T(8,128)(2,1)} fusion(bf16[1024,512]{0,1:T(8,128)(2,1)S(1)} %bitcast.77, bf16[1,1024,7168]{1,2,0:T(8,128)(2,1)} %copy.50, bf16[896,8,4,128]{3,2,1,0:T(4,128)(2,1)} %bitcast.70), kind=kOutput, calls=%fused_computation.5 | convolution fusion | flops 7538212864 | bytes 37748736 | tf_op jit(solution)/shard_map/dot_general | solution.py:39
  235.0 16.6 %fusion.3 = bf16[1,1024,7168]{1,2,0:T(8,128)(2,1)} fusion(bf16[1024,512]{0,1:T(8,128)(2,1)S(1)} %bitcast.78, bf16[1,1024,7168]{1,2,0:T(8,128)(2,1)} %copy.51, bf16[896,8,4,128]{3,2,1,0:T(4,128)(2,1)} %bitcast.71), kind=kOutput, calls=%fused_computation.6 | convolution fusion | flops 7538212864 | bytes 37748736 | tf_op jit(solution)/shard_map/dot_general | solution.py:39
  251.6 20.1 %pad_maximum_fusion = bf16[2,1024,7168]{1,2,0:T(8,128)(2,1)} fusion(bf16[1,1024,7168]{1,2,0:T(8,128)(2,1)} %fusion.3, bf16[1,1024,7168]{1,2,0:T(8,128)(2,1)} %fusion.2), kind=kLoop, calls=%fused_computation | loop fusion | flops 14680064 | bytes 58720256 | tf_op jit(solution)/shard_map/stack | solution.py:58
  271.7 36.2 %copy.49 = bf16[2,1024,7168]{2,1,0:T(8,128)(2,1)} copy(bf16[2,1024,7168]{1,2,0:T(8,128)(2,1)} %pad_maximum_fusion) | data formatting | bytes 58720256 | tf_op jit(solution)/shard_map/stack | solution.py:58
Async XLA Ops:
  6.5 184.2 %all-gather.11.cloned.1.call-start = ((), (), s32[]{:S(2)}) async-start(), calls=%async_computation.5 | async-start | bytes 1310720 | tf_op jit(solution)/shard_map/all_gather | solution.py:28
  19.5 19.2 %all-to-all-start = ((bf16[1,128,8,448]{1,3,0,2:T(8,128)(2,1)}), bf16[1,128,8,448]{1,3,0,2:T(8,128)(2,1)S(1)}, u32[]{:S(2)}, u32[]{:S(2)}) async-start(bf16[1,128,8,448]{1,3,0,2:T(8,128)(2,1)} %bitcast.2), calls=%async_computation | async-start | bytes 1835008 | tf_op jit(solution)/shard_map/all_to_all | solution.py:31
  24.7 167.5 %all-gather.15.cloned.1.call-start = ((), (), s32[]{:S(2)}) async-start(), calls=%async_computation.7 | async-start | bytes 1310720 | tf_op jit(solution)/shard_map/all_gather | solution.py:28
  25.4 168.5 %all-gather.9.cloned.1.call-start = ((), (), s32[]{:S(2)}) async-start(), calls=%async_computation.4 | async-start | bytes 8257536 | tf_op jit(solution)/shard_map/all_gather | solution.py:35
  80.5 125.6 %all-gather.13.cloned.1.call-start = ((), (), s32[]{:S(2)}) async-start(), calls=%async_computation.6 | async-start | bytes 8257536 | tf_op jit(solution)/shard_map/all_gather | solution.py:35
Sparse Core Ops, SparseCore 0:
  8.9 30.6 all-gather.10
  41.2 39.3 all-gather.14
  82.5 52.3 all-gather.8
  136.7 49.8 all-gather.12
